TPU v7x, 256 devices: a whole 4x4x8 slice. The times are simulated.
256 devices in a mesh: dp: 16 (over z, core), expert: 16 (over y, x).
Axes of the slice: x: 4, y: 4, z: 8, core: 2. Of those that a mesh axis runs over, the one named last changes fastest.
Arguments:
- cotangent: bfloat16 [32768, 2048], P(('dp', 'expert')), may hold values from -6 to 6
- saved_gate_up: bfloat16 [32768, 8, 1536], P(('dp', 'expert')), may hold values from -6 to 6
- route_ids: int32 [32768, 8], P(('dp', 'expert')), may hold values from 0 to 31, all different within a row; in each aligned block of 128 rows (0 to 127, 128 to 255, ...) at most 64 rows name the same one
- route_weights: float32 [32768, 8], P(('dp', 'expert')), may hold values from 0.05 to 1
- w_down: bfloat16 [32, 768, 2048], P('expert', 'dp'), may hold values from -0.21875 to 0.21875
Outputs:
- grad_gate_up: bfloat16 [32768, 8, 1536], P(('dp', 'expert'))
- route_grad: float32 [32768, 8], P(('dp', 'expert'))
- grad_down: float32 [32, 768, 2048], P('expert', 'dp')
Inputs may be any that keep to these rules, and one draw needn't show every extreme that they name: `route_ids`: within the rows of one device (aligned blocks of 128 tokens), no expert is named by more than 64 routes, and in every draw some expert is named by exactly 64; the 8 experts of a token are distinct.
All inputs are finite; a program needn't handle non-finite values.
Results may differ from a plain program's by a relative error of at most 0.02.
Values may be sent and summed in bfloat16 or wider, within the bound.
A program may use at most 128 MiB of HBM per device.

v0:
```python
import jax
import jax.numpy as jnp
from jax import lax
from jax.sharding import PartitionSpec as P


def slot_positions(flat_ids, experts, capacity):
    onehot = (flat_ids[:, None] == jnp.arange(experts, dtype=jnp.int32)[None, :]).astype(jnp.int32)
    before = jnp.cumsum(onehot, axis=0) - onehot
    slot = jnp.sum(before * onehot, axis=1)
    return flat_ids * capacity + slot


def local(cotangent, saved_gate_up, route_ids, route_weights, w_down):
    tokens, top = route_ids.shape
    width = cotangent.shape[1]
    hidden_units = saved_gate_up.shape[2] // 2
    owners = lax.axis_size("expert")
    local_experts = w_down.shape[0]
    experts = local_experts * owners
    capacity = min(tokens, 2 * tokens * top // experts)
    routes = tokens * top
    gate = saved_gate_up[:, :, :hidden_units].astype(jnp.float32)
    up = saved_gate_up[:, :, hidden_units:].astype(jnp.float32)
    sig = jax.nn.sigmoid(gate)
    act = gate * sig
    hidden = (act * up).astype(jnp.bfloat16)
    weights = route_weights[:, :, None]
    scaled = (weights * hidden.astype(jnp.float32)).astype(jnp.bfloat16)
    flat_ids = route_ids.reshape(routes)
    position = slot_positions(flat_ids, experts, capacity)
    source = (
        jnp.full((experts * capacity,), routes, jnp.int32)
        .at[position]
        .set(jnp.arange(routes, dtype=jnp.int32))
    )
    dy_rows = jnp.concatenate([cotangent, jnp.zeros((1, width), cotangent.dtype)], 0)[source // top]
    h_rows = jnp.concatenate(
        [scaled.reshape(routes, hidden_units), jnp.zeros((1, hidden_units), jnp.bfloat16)], 0
    )[source]
    dy_send = dy_rows.reshape(owners, local_experts, capacity, width)
    h_send = h_rows.reshape(owners, local_experts, capacity, hidden_units)
    full_down = lax.all_gather(w_down, "dp", axis=1, tiled=True)
    dy_recv, h_recv = (
        lax.all_to_all(dy_send, "expert", split_axis=0, concat_axis=2, tiled=True),
        lax.all_to_all(h_send, "expert", split_axis=0, concat_axis=2, tiled=True),
    )
    dy_recv = dy_recv[0]
    h_recv = h_recv[0]
    grads = jnp.einsum(
        "jsd,jfd->jsf", dy_recv, full_down, preferred_element_type=jnp.float32
    ).astype(jnp.bfloat16)
    back = lax.all_to_all(
        grads.reshape(1, local_experts, owners * capacity, hidden_units),
        "expert",
        split_axis=2,
        concat_axis=0,
        tiled=True,
    )
    summed = lax.psum_scatter(
        jnp.einsum("jsn,jsd->njd", h_recv, dy_recv, preferred_element_type=jnp.float32).astype(
            jnp.bfloat16
        ),
        "dp",
        scatter_dimension=0,
        tiled=True,
    ).astype(jnp.float32)
    grad_down = jnp.transpose(summed, (1, 0, 2))
    returned_rows = back.reshape(experts * capacity, hidden_units)[position]
    qf = returned_rows.reshape(tokens, top, hidden_units).astype(jnp.float32)
    route_grad = jnp.sum(qf * hidden.astype(jnp.float32), -1)
    d_hidden = weights * qf
    d_gate = d_hidden * up * sig * (1.0 + gate * (1.0 - sig))
    d_up = d_hidden * act
    grad_gate_up = jnp.concatenate([d_gate, d_up], -1).astype(jnp.bfloat16)
    return (grad_gate_up, route_grad, grad_down)


def solution(mesh):
    return jax.shard_map(
        local,
        mesh=mesh,
        in_specs=(
            P(("dp", "expert"), None),
            P(("dp", "expert"), None, None),
            P(("dp", "expert"), None),
            P(("dp", "expert"), None),
            P("expert", "dp", None),
        ),
        out_specs=(
            P(("dp", "expert"), None, None),
            P(("dp", "expert"), None),
            P("expert", "dp", None),
        ),
        check_vma=False,
    )
```

profile of v0, /device:TPU:2, one launch (start us, length us, event | category | flops | bytes accessed | tf_op | source)
XLA Modules:
  0.0 447.5 jit_solution(13268947145808185518)
XLA Ops:
  7.2 0.7 all-gather.2.cloned.1.call-update
  7.9 0.8 copy.27
  8.9 0.7 broadcast_multiply_fusion
  9.8 9.0 %reduce-window.6 = s32[32,8,128]{2,1,0:T(8,128)S(1)} reduce-window(s32[32,8,128]{2,1,0:T(8,128)S(1)} %fusion.16, s32[]{:T(128)} %constant.16.clone.1), window={size=1x1x128 pad=0_0x0_0x127_0}, to_apply=%region_0.0 | reduce-window | flops 4161536 | bytes 262148 | tf_op jit(solution)/shard_map/reduce-window
  18.9 0.1 copy.29
  19.1 1.1 concatenate.10
  20.4 4.3 scatter_custom_fusion
  24.8 11.0 %gather_fusion = bf16[2048,2048]{1,0:T(8,128)(2,1)} fusion(bf16[129,2048]{1,0:T(8,128)(2,1)S(1)} %concatenate.10, s32[2048]{0:T(1024)S(1)} %get-tuple-element.19), kind=kCustom, calls=%fused_computation | custom fusion | bytes 16785408 | tf_op jit(solution)/shard_map/gather | solution.py:37
  35.8 102.0 %all_to_all.45 = bf16[16,2,64,2048]{3,2,1,0:T(8,128)(2,1)} all-to-all(bf16[16,2,64,2048]{3,2,1,0:T(8,128)(2,1)} %bitcast.53), channel_id=1, replica_groups=mesh['dp'=16,'expert'=16] {'expert'}, dimensions={0} | all-to-all | bytes 16777216 | tf_op jit(solution)/shard_map/all_to_all | solution.py:45
  137.8 8.3 %copy.31 = bf16[1,2,16,64,2048]{4,3,2,1,0:T(8,128)(2,1)} copy(bf16[1,2,16,64,2048]{4,3,1,2,0:T(8,128)(2,1)} %bitcast.54) | data formatting | bytes 16777216 | tf_op jit(solution)/shard_map/all_to_all | solution.py:45
  146.0 11.0 %convert_bitcast_fusion.1 = bf16[1,2,1024,768]{3,2,1,0:T(8,128)(2,1)S(1)} fusion(bf16[2,1024,2048]{2,1,0:T(8,128)(2,1)} %bitcast.58, bf16[2,768,2048]{2,1,0:T(8,128)(2,1)} %all-gather.2.cloned.1.call-done), kind=kOutput, calls=%fused_computation.26 | convolution fusion | flops 6444023808 | bytes 17825792 | tf_op jit(solution)/shard_map/jsd,jfd->jsf/dot_general | solution.py:50
  157.1 4.9 %copy.32 = bf16[1,2,1024,768]{3,1,0,2:T(2,128)(2,1)} copy(bf16[1,2,1024,768]{3,2,1,0:T(8,128)(2,1)S(1)} %convert_bitcast_fusion.1) | data formatting | bytes 6291456 | tf_op jit(solution)/shard_map/reshape | solution.py:54
  162.0 5.1 %all-to-all-start.1 = ((bf16[1,2,1024,768]{3,1,0,2:T(2,128)(2,1)}), bf16[1,2,1024,768]{3,1,0,2:T(2,128)(2,1)S(1)}, u32[]{:S(2)}, u32[]{:S(2)}) async-start(bf16[1,2,1024,768]{3,1,0,2:T(2,128)(2,1)} %copy.32), calls=%async_computation.1 | async-start | bytes 6291456 | tf_op jit(solution)/shard_map/all_to_all | solution.py:53
  167.1 0.2 all-reduce.5.cloned.1.call-start
  167.4 38.9 %all-to-all-done.1 = bf16[1,2,1024,768]{3,1,0,2:T(2,128)(2,1)S(1)} async-done(((bf16[1,2,1024,768]{3,1,0,2:T(2,128)(2,1)}), bf16[1,2,1024,768]{3,1,0,2:T(2,128)(2,1)S(1)}, u32[]{:S(2)}, u32[]{:S(2)}) %all-to-all-start.1) | async-done | bytes 3145760 | tf_op jit(solution)/shard_map/all_to_all | solution.py:53
  206.3 1.7 copy-done.1
  207.9 2.5 copy.33
  210.5 5.2 %gather_fusion.1 = bf16[1024,768]{1,0:T(8,128)(2,1)} fusion(bf16[2048,768]{1,0:T(8,128)(2,1)S(1)} %bitcast.52, s32[1024]{0:T(1024)S(1)} %broadcast_clamp_fusion), kind=kCustom, calls=%fused_computation.1 | custom fusion | bytes 3149824 | tf_op jit(solution)/shard_map/gather | solution.py:69
  215.7 5.0 %fusion.12 = (bf16[1024,768]{1,0:T(8,128)(2,1)S(1)}, bf16[128,8,768]{2,1,0:T(8,128)(2,1)S(1)}, bf16[128,8,768]{2,1,0:T(8,128)(2,1)}, bf16[128,8,768]{2,1,0:T(8,128)(2,1)}) fusion(f32[128,8]{1,0:T(8,128)S(1)} %copy.25, bf16[128,8,1536]{2,1,0:T(8,128)(2,1)} %param.6, bf16[1024,768]{1,0:T(8,128)(2,1)} %gather_fusion.1), kind=kLoop, calls=%fused_computation.27 | loop fusion | flops 17301504 | bytes 11014144 | tf_op jit(solution)/shard_map/reshape | solution.py:39
  220.8 9.4 %gather_fusion.2 = bf16[2048,768]{1,0:T(8,128)(2,1)} fusion(bf16[1025,768]{1,0:T(8,128)(2,1)S(1)} %concatenate.12, s32[2048]{0:T(1024)S(1)} %get-tuple-element.18), kind=kCustom, calls=%fused_computation.2 | custom fusion | bytes 6299648 | tf_op jit(solution)/shard_map/gather | solution.py:38
  230.2 47.8 %all_to_all.46 = bf16[16,2,64,768]{3,2,1,0:T(8,128)(2,1)S(1)} all-to-all(bf16[16,2,64,768]{3,2,1,0:T(8,128)(2,1)} %bitcast.57), channel_id=1, replica_groups=mesh['dp'=16,'expert'=16] {'expert'}, dimensions={0} | all-to-all | bytes 6291456 | tf_op jit(solution)/shard_map/all_to_all | solution.py:46
  278.0 0.2 copy.34
  278.2 15.2 %convert_bitcast_fusion = bf16[768,2,2048]{0,2,1:T(8,128)(2,1)} fusion(bf16[2,1024,2048]{2,1,0:T(8,128)(2,1)} %bitcast.59, bf16[2,1024,768]{2,1,0:T(8,128)(2,1)S(1)} %bitcast.60), kind=kOutput, calls=%fused_computation.4 | convolution fusion | flops 6445596672 | bytes 17825792 | tf_op jit(solution)/shard_map/jsn,jsd->njd/dot_general | solution.py:61
  293.4 16.4 %copy.36 = bf16[768,2,2048]{2,1,0:T(2,128)(2,1)} copy(bf16[768,2,2048]{0,2,1:T(8,128)(2,1)} %convert_bitcast_fusion) | data formatting | bytes 12582912 | tf_op jit(solution)/shard_map/convert_element_type | solution.py:61
  309.8 0.6 copy-done.3
  310.4 0.6 dynamic-slice
  311.7 0.5 fusion.7
  312.2 0.7 copy.37
  312.8 3.8 pad_maximum_fusion
  316.6 121.3 %all-reduce.5.cloned.1.call-done = bf16[768,2,2048]{2,1,0:T(2,128)(2,1)} async-done(((bf16[768,2,2048]{2,1,0:T(2,128)(2,1)}), bf16[768,2,2048]{2,1,0:T(2,128)(2,1)}) %all-reduce.5.cloned.1.call-update) | async-done | bytes 6291472
  437.9 1.4 convert_bitcast_fusion.2
  439.3 1.3 copy.38
  (26 shorter events, 1.0 us)
Async XLA Ops:
  7.2 138.9 %all-gather.2.cloned.1.call-start = ((), (), s32[]{:S(2)}) async-start(), calls=%async_computation.3 | async-start | bytes 6684672 | tf_op jit(solution)/shard_map/all_gather | solution.py:43
  162.0 5.3 %copy-start.2 = (f32[128,8]{0,1:T(8,128)S(1)}, f32[128,8]{0,1:T(8,128)}, u32[]{:S(2)}) copy-start(f32[128,8]{0,1:T(8,128)} %param.8) | copy-start | bytes 12292
  162.0 44.3 %all-to-all-start.1 = ((bf16[1,2,1024,768]{3,1,0,2:T(2,128)(2,1)}), bf16[1,2,1024,768]{3,1,0,2:T(2,128)(2,1)S(1)}, u32[]{:S(2)}, u32[]{:S(2)}) async-start(bf16[1,2,1024,768]{3,1,0,2:T(2,128)(2,1)} %copy.32), calls=%async_computation.1 | async-start | bytes 6291456 | tf_op jit(solution)/shard_map/all_to_all | solution.py:53
  167.1 270.8 %all-reduce.5.cloned.1.call-start = ((), (), s32[]{:S(2)}) async-start(), calls=%async_computation.4 | async-start | bytes 12582912
  206.3 1.7 copy-start.1
  309.8 0.7 copy-start.3
  309.8 1.9 copy-start
Sparse Core Ops, SparseCore 0:
  9.8 48.9 all-gather.1
  309.9 127.9 all-reduce.4
where the time goes:
time: 448 us; the launch traced here: 447 us
  waiting for transfers between devices  161 us (36%)
  blocking collectives  150 us (33%)
  local copies, waits for them, and re-layouts  69.9 us (16%)
  matrix products  26.2 us (6%)
  other arithmetic  20.6 us (5%)
  between operations  14.8 us (3%)
  starting transfers between devices  5.37 us (1%)
    unnamed x3, waiting for transfers between devices  122 us
    all_to_all x1, blocking collectives, local(): lax.all_to_all(dy_send, 'expert', split_axis=0, concat_axis=2, tiled=True)  102 us
    all_to_all x1, blocking collectives, local(): lax.all_to_all(h_send, 'expert', split_axis=0, concat_axis=2, tiled=True)  47.8 us
    all_to_all x1, waiting for transfers between devices, local(): lax.all_to_all(grads.reshape(1, local_experts, owners * capacity, hidden_...  38.9 us
    convert_element_type x1, local copies, waits for them, and re-layouts, local(): jnp.einsum('jsn,jsd->njd', h_recv, dy_recv, preferred_element_type=jnp.fl...  16.4 us
    dot_general x1, matrix products, local(): jnp.einsum('jsn,jsd->njd', h_recv, dy_recv, preferred_element_type=jnp.fl...  15.2 us
    gather x1, local copies, waits for them, and re-layouts, local(): jnp.concatenate([cotangent, jnp.zeros((1, width), cotangent.dtype)], 0)  11 us
    dot_general x1, matrix products, local(): jnp.einsum('jsd,jfd->jsf', dy_recv, full_down, preferred_element_type=jnp...  11 us
  transfers between devices with their start and end apart: 3, of which 2 were waited for; matrix products, arithmetic and copies ran while one was open for 9% of the time, Pallas kernels for 0%

commit v1 on v0

--- a/solution.py
+++ b/solution.py
@@ -2,6 +2,22 @@
 import jax.numpy as jnp
 from jax import lax
 from jax.sharding import PartitionSpec as P
+
+
+def exchange_in_pairs(x, axis, split, join):
+    ways, here = (lax.axis_size(axis), lax.axis_index(axis))
+    width = x.shape[split] // ways
+    dims = list(x.shape)
+    dims[split] = width
+    height = dims[join]
+    dims[join] = height * ways
+    full = jnp.zeros(dims, x.dtype)
+    for mask in range(ways):
+        part = lax.dynamic_slice_in_dim(x, (here ^ mask) * width, width, axis=split)
+        if mask:
+            part = lax.ppermute(part, axis, [(d, d ^ mask) for d in range(ways)])
+        full = lax.dynamic_update_slice_in_dim(full, part, (here ^ mask) * height, axis=join)
+    return full
 
 
 def slot_positions(flat_ids, experts, capacity):
@@ -50,12 +66,8 @@
     grads = jnp.einsum(
         "jsd,jfd->jsf", dy_recv, full_down, preferred_element_type=jnp.float32
     ).astype(jnp.bfloat16)
-    back = lax.all_to_all(
-        grads.reshape(1, local_experts, owners * capacity, hidden_units),
-        "expert",
-        split_axis=2,
-        concat_axis=0,
-        tiled=True,
+    back = exchange_in_pairs(
+        grads.reshape(1, local_experts, owners * capacity, hidden_units), "expert", 2, 0
     )
     summed = lax.psum_scatter(
         jnp.einsum("jsn,jsd->njd", h_recv, dy_recv, preferred_element_type=jnp.float32).astype(

time: 448 us -> 480 us (1.071)
  blocking collectives: 150 us -> 39.9 us
  waiting for transfers between devices: 161 us -> 255 us
  starting transfers between devices: 5.37 us -> 55.9 us
    all_to_all x1 -> x0, blocking collectives: 102 us -> none  [local(): lax.all_to_all(dy_send, 'expert', split_axis=0, concat_axis=2, tiled=True)]
    all_to_all x1, waiting for transfers between devices: 38.9 us -> 121 us  [local(): lax.all_to_all(dy_send, 'expert', split_axis=0, concat_axis=2, tiled=True)]
    ppermute x0 -> x15, starting transfers between devices: none -> 48.3 us  [exchange_in_pairs(): part = lax.ppermute(part, axis, [(d, d ^ mask) for d in range(ways)])]
    ppermute x0 -> x15, waiting for transfers between devices: none -> 12.1 us  [exchange_in_pairs(): part = lax.ppermute(part, axis, [(d, d ^ mask) for d in range(ways)])]
    all_to_all x1, blocking collectives: 47.8 us -> 39.9 us  [local(): lax.all_to_all(h_send, 'expert', split_axis=0, concat_axis=2, tiled=True)]
    reshape x1 -> x0, local copies, waits for them, and re-layouts: 4.9 us -> none  [local(): grads.reshape(1, local_experts, owners * capacity, hidden_units)]
  transfers between devices with their start and end apart: 3 -> 18, of which waited for: 2 -> 8; matrix products, arithmetic and copies ran while one was open for 9% -> 9% of each run, Pallas kernels for 0% -> 0%
where the time goes in v1:
time: 480 us; the launch traced here: 479 us
  waiting for transfers between devices  255 us (53%)
  local copies, waits for them, and re-layouts  66.6 us (14%)
  starting transfers between devices  55.9 us (12%)
  blocking collectives  39.9 us (8%)
  matrix products  26.2 us (5%)
  other arithmetic  20.6 us (4%)
  between operations  15.3 us (3%)
    unnamed x3, waiting for transfers between devices  122 us
    all_to_all x1, waiting for transfers between devices, local(): lax.all_to_all(dy_send, 'expert', split_axis=0, concat_axis=2, tiled=True)  121 us
    ppermute x15, starting transfers between devices, exchange_in_pairs(): part = lax.ppermute(part, axis, [(d, d ^ mask) for d in range(ways)])  48.3 us
    all_to_all x1, blocking collectives, local(): lax.all_to_all(h_send, 'expert', split_axis=0, concat_axis=2, tiled=True)  39.9 us
    convert_element_type x1, local copies, waits for them, and re-layouts, local(): jnp.einsum('jsn,jsd->njd', h_recv, dy_recv, preferred_element_type=jnp.fl...  16.4 us
    dot_general x1, matrix products, local(): jnp.einsum('jsn,jsd->njd', h_recv, dy_recv, preferred_element_type=jnp.fl...  15.2 us
    ppermute x15, waiting for transfers between devices, exchange_in_pairs(): part = lax.ppermute(part, axis, [(d, d ^ mask) for d in range(ways)])  12.1 us
    dot_general x1, matrix products, local(): jnp.einsum('jsd,jfd->jsf', dy_recv, full_down, preferred_element_type=jnp...  11 us
  transfers between devices with their start and end apart: 18, of which 8 were waited for; matrix products, arithmetic and copies ran while one was open for 9% of the time, Pallas kernels for 0%

profile of v1, /device:TPU:2, one launch (start us, length us, event | category | flops | bytes accessed | tf_op | source)
XLA Modules:
  0.0 479.2 jit_solution(3963954701931915510)
XLA Ops:
  9.8 9.0 %reduce-window.6 = s32[32,8,128]{2,1,0:T(8,128)S(1)} reduce-window(s32[32,8,128]{2,1,0:T(8,128)S(1)} %fusion.16, s32[]{:T(128)} %constant.30.clone.1), window={size=1x1x128 pad=0_0x0_0x127_0}, to_apply=%region_0.0 | reduce-window | flops 4161536 | bytes 262148 | tf_op jit(solution)/shard_map/reduce-window
  20.4 4.3 scatter_custom_fusion
  24.8 11.0 %gather_fusion = bf16[2048,2048]{1,0:T(8,128)(2,1)} fusion(bf16[129,2048]{1,0:T(8,128)(2,1)S(1)} %concatenate.10, s32[2048]{0:T(1024)S(1)} %get-tuple-element.34), kind=kCustom, calls=%fused_computation | custom fusion | bytes 16785408 | tf_op jit(solution)/shard_map/gather | solution.py:53
  35.7 7.5 %all-to-all-start = ((bf16[16,2,64,2048]{3,2,1,0:T(8,128)(2,1)}), bf16[16,2,64,2048]{3,2,1,0:T(8,128)(2,1)}, u32[]{:S(2)}, u32[]{:S(2)}) async-start(bf16[16,2,64,2048]{3,2,1,0:T(8,128)(2,1)} %bitcast.80), calls=%async_computation | async-start | bytes 16777216 | tf_op jit(solution)/shard_map/all_to_all | solution.py:61
  43.4 120.7 %all-to-all-done = bf16[16,2,64,2048]{3,2,1,0:T(8,128)(2,1)} async-done(((bf16[16,2,64,2048]{3,2,1,0:T(8,128)(2,1)}), bf16[16,2,64,2048]{3,2,1,0:T(8,128)(2,1)}, u32[]{:S(2)}, u32[]{:S(2)}) %all-to-all-start) | async-done | bytes 8388640 | tf_op jit(solution)/shard_map/all_to_all | solution.py:61
  164.0 8.3 %copy.29 = bf16[1,2,16,64,2048]{4,3,2,1,0:T(8,128)(2,1)} copy(bf16[1,2,16,64,2048]{4,3,1,2,0:T(8,128)(2,1)} %bitcast.6) | data formatting | bytes 16777216 | tf_op jit(solution)/shard_map/all_to_all | solution.py:61
  172.3 11.0 %convolution_convert_fusion = bf16[2,1024,768]{2,1,0:T(8,128)(2,1)S(1)} fusion(bf16[2,1024,2048]{2,1,0:T(8,128)(2,1)} %bitcast.83, bf16[2,768,2048]{2,1,0:T(8,128)(2,1)} %all-gather.2.cloned.1.call-done), kind=kOutput, calls=%fused_computation.26 | convolution fusion | flops 6444023808 | bytes 17825792 | tf_op jit(solution)/shard_map/jsd,jfd->jsf/dot_general | solution.py:66
  183.4 1.7 copy-done.1
  185.0 1.5 dynamic-slice_bitcast_fusion
  186.6 3.3 collective-permute-start
  192.7 3.7 collective-permute-start.4
  200.4 1.6 collective-permute-start.6
  202.0 3.0 collective-permute-start.7
  205.0 14.6 %collective-permute-start.8 = (bf16[1,2,64,768]{3,2,1,0:T(8,128)(2,1)S(1)}, bf16[1,2,64,768]{3,2,1,0:T(8,128)(2,1)S(1)}, u32[]{:S(2)}, u32[]{:S(2)}) collective-permute-start(bf16[1,2,64,768]{3,2,1,0:T(8,128)(2,1)S(1)} %copy-done.7), channel_id=1, source_target_pairs={{0,9},{1,8},{2,11},{3,10},{4,13},{5,12},{6,15},{7,14},{8,1},{9,0},... | collective-permute-start | bytes 589832 | tf_op jit(solution)/shard_map/ppermute | solution.py:18
  219.7 8.7 %collective-permute-start.9 = (bf16[1,2,64,768]{3,2,1,0:T(8,128)(2,1)S(1)}, bf16[1,2,64,768]{3,2,1,0:T(8,128)(2,1)S(1)}, u32[]{:S(2)}, u32[]{:S(2)}) collective-permute-start(bf16[1,2,64,768]{3,2,1,0:T(8,128)(2,1)S(1)} %copy-done.6), channel_id=1, source_target_pairs={{0,10},{1,11},{2,8},{3,9},{4,14},{5,15},{6,12},{7,13},{8,2},{9,3},... | collective-permute-start | bytes 589832 | tf_op jit(solution)/shard_map/ppermute | solution.py:18
  228.7 3.9 collective-permute-start.12
  232.7 6.0 %collective-permute-start.13 = (bf16[1,2,64,768]{3,2,1,0:T(8,128)(2,1)S(1)}, bf16[1,2,64,768]{3,2,1,0:T(8,128)(2,1)S(1)}, u32[]{:S(2)}, u32[]{:S(2)}) collective-permute-start(bf16[1,2,64,768]{3,2,1,0:T(8,128)(2,1)S(1)} %copy-done.2), channel_id=1, source_target_pairs={{0,14},{1,15},{2,12},{3,13},{4,10},{5,11},{6,8},{7,9},{8,6},{9,7},... | collective-permute-start | bytes 589832 | tf_op jit(solution)/shard_map/ppermute | solution.py:18
  238.7 1.8 collective-permute-done.9
  240.5 3.5 collective-permute-done.10
  244.0 1.7 collective-permute-done.11
  245.8 2.1 collective-permute-done.13
  248.0 2.0 collective-permute-done.14
  250.0 5.2 %gather_fusion.1 = bf16[1024,768]{1,0:T(8,128)(2,1)} fusion(bf16[2048,768]{1,0:T(8,128)(2,1)S(1)} %bitcast.79, s32[1024]{0:T(1024)S(1)} %broadcast_clamp_fusion), kind=kCustom, calls=%fused_computation.1 | custom fusion | bytes 3149824 | tf_op jit(solution)/shard_map/gather | solution.py:81
  255.2 5.0 %fusion.12 = (bf16[1024,768]{1,0:T(8,128)(2,1)S(1)}, bf16[128,8,768]{2,1,0:T(8,128)(2,1)S(1)}, bf16[128,8,768]{2,1,0:T(8,128)(2,1)}, bf16[128,8,768]{2,1,0:T(8,128)(2,1)}) fusion(f32[128,8]{1,0:T(8,128)S(1)} %copy.23, bf16[128,8,1536]{2,1,0:T(8,128)(2,1)} %param.6, bf16[1024,768]{1,0:T(8,128)(2,1)} %gather_fusion.1), kind=kLoop, calls=%fused_computation.27 | loop fusion | flops 17301504 | bytes 11014144 | tf_op jit(solution)/shard_map/reshape | solution.py:55
  260.4 9.4 %gather_fusion.2 = bf16[2048,768]{1,0:T(8,128)(2,1)} fusion(bf16[1025,768]{1,0:T(8,128)(2,1)S(1)} %concatenate.12, s32[2048]{0:T(1024)S(1)} %get-tuple-element.33), kind=kCustom, calls=%fused_computation.2 | custom fusion | bytes 6299648 | tf_op jit(solution)/shard_map/gather | solution.py:54
  269.8 39.9 %all_to_all.30 = bf16[16,2,64,768]{3,2,1,0:T(8,128)(2,1)S(1)} all-to-all(bf16[16,2,64,768]{3,2,1,0:T(8,128)(2,1)} %bitcast.82), channel_id=1, replica_groups=mesh['dp'=16,'expert'=16] {'expert'}, dimensions={0} | all-to-all | bytes 6291456 | tf_op jit(solution)/shard_map/all_to_all | solution.py:62
  309.9 15.2 %convert_bitcast_fusion = bf16[768,2,2048]{0,2,1:T(8,128)(2,1)} fusion(bf16[2,1024,2048]{2,1,0:T(8,128)(2,1)} %bitcast.84, bf16[2,1024,768]{2,1,0:T(8,128)(2,1)S(1)} %bitcast.85), kind=kOutput, calls=%fused_computation.4 | convolution fusion | flops 6445596672 | bytes 17825792 | tf_op jit(solution)/shard_map/jsn,jsd->njd/dot_general | solution.py:73
  325.1 16.4 %copy.32 = bf16[768,2,2048]{2,1,0:T(2,128)(2,1)} copy(bf16[768,2,2048]{0,2,1:T(8,128)(2,1)} %convert_bitcast_fusion) | data formatting | bytes 12582912 | tf_op jit(solution)/shard_map/convert_element_type | solution.py:73
  344.6 3.8 pad_maximum_fusion
  348.3 121.2 %all-reduce.5.cloned.1.call-done = bf16[768,2,2048]{2,1,0:T(2,128)(2,1)} async-done(((bf16[768,2,2048]{2,1,0:T(2,128)(2,1)}), bf16[768,2,2048]{2,1,0:T(2,128)(2,1)}) %all-reduce.5.cloned.1.call-update) | async-done | bytes 6291472
  469.6 1.4 convert_bitcast_fusion.1
  471.0 1.3 copy.34
  (89 shorter events, 14.0 us)
Async XLA Ops:
  7.2 165.2 %all-gather.2.cloned.1.call-start = ((), (), s32[]{:S(2)}) async-start(), calls=%async_computation.2 | async-start | bytes 6684672 | tf_op jit(solution)/shard_map/all_gather | solution.py:59
  35.7 128.3 %all-to-all-start = ((bf16[16,2,64,2048]{3,2,1,0:T(8,128)(2,1)}), bf16[16,2,64,2048]{3,2,1,0:T(8,128)(2,1)}, u32[]{:S(2)}, u32[]{:S(2)}) async-start(bf16[16,2,64,2048]{3,2,1,0:T(8,128)(2,1)} %bitcast.80), calls=%async_computation | async-start | bytes 16777216 | tf_op jit(solution)/shard_map/all_to_all | solution.py:61
  43.2 426.4 %all-reduce.5.cloned.1.call-start = ((), (), s32[]{:S(2)}) async-start(), calls=%async_computation.3 | async-start | bytes 12582912
  183.3 1.7 copy-start.1
  185.0 4.9 %copy-start.11 = (f32[128,8]{0,1:T(8,128)S(1)}, f32[128,8]{0,1:T(8,128)}, u32[]{:S(2)}) copy-start(f32[128,8]{0,1:T(8,128)} %param.8) | copy-start | bytes 12292
  186.6 11.1 %collective-permute-start = (bf16[1,2,64,768]{3,2,1,0:T(8,128)(2,1)}, bf16[1,2,64,768]{3,2,1,0:T(8,128)(2,1)}, u32[]{:S(2)}, u32[]{:S(2)}) collective-permute-start(bf16[1,2,64,768]{3,2,1,0:T(8,128)(2,1)} %get-tuple-element.32), channel_id=1, source_target_pairs={{0,1},{1,0},{2,3},{3,2},{4,5},{5,4},{6,7},{7,6},{8,9},{9,8},{10,11... | collective-permute-start | bytes 589832 | tf_op jit(solution)/shard_map/ppermute | solution.py:18
  190.1 7.7 %copy-start.10 = (bf16[1,2,64,768]{3,2,1,0:T(8,128)(2,1)S(1)}, bf16[1,2,64,768]{3,2,1,0:T(8,128)(2,1)}, u32[]{:S(2)}) copy-start(bf16[1,2,64,768]{3,2,1,0:T(8,128)(2,1)} %get-tuple-element.27) | copy-start | bytes 589828
  190.1 10.3 %copy-start.9 = (bf16[1,2,64,768]{3,2,1,0:T(8,128)(2,1)S(1)}, bf16[1,2,64,768]{3,2,1,0:T(8,128)(2,1)}, u32[]{:S(2)}) copy-start(bf16[1,2,64,768]{3,2,1,0:T(8,128)(2,1)} %get-tuple-element.26) | copy-start | bytes 589828
  190.1 11.9 %copy-start.8 = (bf16[1,2,64,768]{3,2,1,0:T(8,128)(2,1)S(1)}, bf16[1,2,64,768]{3,2,1,0:T(8,128)(2,1)}, u32[]{:S(2)}) copy-start(bf16[1,2,64,768]{3,2,1,0:T(8,128)(2,1)} %get-tuple-element.25) | copy-start | bytes 589828
  190.1 14.9 %copy-start.7 = (bf16[1,2,64,768]{3,2,1,0:T(8,128)(2,1)S(1)}, bf16[1,2,64,768]{3,2,1,0:T(8,128)(2,1)}, u32[]{:S(2)}) copy-start(bf16[1,2,64,768]{3,2,1,0:T(8,128)(2,1)} %get-tuple-element.24) | copy-start | bytes 589828
  190.1 29.5 %copy-start.6 = (bf16[1,2,64,768]{3,2,1,0:T(8,128)(2,1)S(1)}, bf16[1,2,64,768]{3,2,1,0:T(8,128)(2,1)}, u32[]{:S(2)}) copy-start(bf16[1,2,64,768]{3,2,1,0:T(8,128)(2,1)} %get-tuple-element.23) | copy-start | bytes 589828
  190.1 38.3 %copy-start.5 = (bf16[1,2,64,768]{3,2,1,0:T(8,128)(2,1)S(1)}, bf16[1,2,64,768]{3,2,1,0:T(8,128)(2,1)}, u32[]{:S(2)}) copy-start(bf16[1,2,64,768]{3,2,1,0:T(8,128)(2,1)} %get-tuple-element.22) | copy-start | bytes 589828
  190.1 38.4 %copy-start.4 = (bf16[1,2,64,768]{3,2,1,0:T(8,128)(2,1)S(1)}, bf16[1,2,64,768]{3,2,1,0:T(8,128)(2,1)}, u32[]{:S(2)}) copy-start(bf16[1,2,64,768]{3,2,1,0:T(8,128)(2,1)} %get-tuple-element.21) | copy-start | bytes 589828
  190.1 10.2 %collective-permute-start.1 = (bf16[1,2,64,768]{3,2,1,0:T(8,128)(2,1)}, bf16[1,2,64,768]{3,2,1,0:T(8,128)(2,1)S(1)}, u32[]{:S(2)}, u32[]{:S(2)}) collective-permute-start(bf16[1,2,64,768]{3,2,1,0:T(8,128)(2,1)} %get-tuple-element.31), channel_id=1, source_target_pairs={{0,2},{1,3},{2,0},{3,1},{4,6},{5,7},{6,4},{7,5},{8,10},{9,11},{10,... | collective-permute-start | bytes 589832 | tf_op jit(solution)/shard_map/ppermute | solution.py:18
  191.0 11.0 %collective-permute-start.2 = (bf16[1,2,64,768]{3,2,1,0:T(8,128)(2,1)}, bf16[1,2,64,768]{3,2,1,0:T(8,128)(2,1)S(1)}, u32[]{:S(2)}, u32[]{:S(2)}) collective-permute-start(bf16[1,2,64,768]{3,2,1,0:T(8,128)(2,1)} %get-tuple-element.30), channel_id=1, source_target_pairs={{0,3},{1,2},{2,1},{3,0},{4,7},{5,6},{6,5},{7,4},{8,11},{9,10},{10,... | collective-permute-start | bytes 589832 | tf_op jit(solution)/shard_map/ppermute | solution.py:18
  191.8 13.2 %collective-permute-start.3 = (bf16[1,2,64,768]{3,2,1,0:T(8,128)(2,1)}, bf16[1,2,64,768]{3,2,1,0:T(8,128)(2,1)S(1)}, u32[]{:S(2)}, u32[]{:S(2)}) collective-permute-start(bf16[1,2,64,768]{3,2,1,0:T(8,128)(2,1)} %get-tuple-element.29), channel_id=1, source_target_pairs={{0,4},{1,5},{2,6},{3,7},{4,0},{5,1},{6,2},{7,3},{8,12},{9,13},{10,... | collective-permute-start | bytes 589832 | tf_op jit(solution)/shard_map/ppermute | solution.py:18
  192.7 36.0 %copy-start.3 = (bf16[1,2,64,768]{3,2,1,0:T(8,128)(2,1)S(1)}, bf16[1,2,64,768]{3,2,1,0:T(8,128)(2,1)}, u32[]{:S(2)}) copy-start(bf16[1,2,64,768]{3,2,1,0:T(8,128)(2,1)} %get-tuple-element.20) | copy-start | bytes 589828
  192.7 39.9 %copy-start.2 = (bf16[1,2,64,768]{3,2,1,0:T(8,128)(2,1)S(1)}, bf16[1,2,64,768]{3,2,1,0:T(8,128)(2,1)}, u32[]{:S(2)}) copy-start(bf16[1,2,64,768]{3,2,1,0:T(8,128)(2,1)} %get-tuple-element.19) | copy-start | bytes 589828
  192.7 26.9 %collective-permute-start.4 = (bf16[1,2,64,768]{3,2,1,0:T(8,128)(2,1)}, bf16[1,2,64,768]{3,2,1,0:T(8,128)(2,1)S(1)}, u32[]{:S(2)}, u32[]{:S(2)}) collective-permute-start(bf16[1,2,64,768]{3,2,1,0:T(8,128)(2,1)} %get-tuple-element.28), channel_id=1, source_target_pairs={{0,5},{1,4},{2,7},{3,6},{4,1},{5,0},{6,3},{7,2},{8,13},{9,12},{10,... | collective-permute-start | bytes 589832 | tf_op jit(solution)/shard_map/ppermute | solution.py:18
  197.7 30.7 %collective-permute-start.5 = (bf16[1,2,64,768]{3,2,1,0:T(8,128)(2,1)S(1)}, bf16[1,2,64,768]{3,2,1,0:T(8,128)(2,1)S(1)}, u32[]{:S(2)}, u32[]{:S(2)}) collective-permute-start(bf16[1,2,64,768]{3,2,1,0:T(8,128)(2,1)S(1)} %copy-done.10), channel_id=1, source_target_pairs={{0,6},{1,7},{2,4},{3,5},{4,2},{5,3},{6,0},{7,1},{8,14},{9,15},{10,... | collective-permute-start | bytes 589832 | tf_op jit(solution)/shard_map/ppermute | solution.py:18
  200.4 28.2 %collective-permute-start.6 = (bf16[1,2,64,768]{3,2,1,0:T(8,128)(2,1)S(1)}, bf16[1,2,64,768]{3,2,1,0:T(8,128)(2,1)S(1)}, u32[]{:S(2)}, u32[]{:S(2)}) collective-permute-start(bf16[1,2,64,768]{3,2,1,0:T(8,128)(2,1)S(1)} %copy-done.9), channel_id=1, source_target_pairs={{0,7},{1,6},{2,5},{3,4},{4,3},{5,2},{6,1},{7,0},{8,15},{9,14},{10,... | collective-permute-start | bytes 589832 | tf_op jit(solution)/shard_map/ppermute | solution.py:18
  202.0 26.7 %collective-permute-start.7 = (bf16[1,2,64,768]{3,2,1,0:T(8,128)(2,1)S(1)}, bf16[1,2,64,768]{3,2,1,0:T(8,128)(2,1)S(1)}, u32[]{:S(2)}, u32[]{:S(2)}) collective-permute-start(bf16[1,2,64,768]{3,2,1,0:T(8,128)(2,1)S(1)} %copy-done.8), channel_id=1, source_target_pairs={{0,8},{1,9},{2,10},{3,11},{4,12},{5,13},{6,14},{7,15},{8,0},{9,1},... | collective-permute-start | bytes 589832 | tf_op jit(solution)/shard_map/ppermute | solution.py:18
  205.0 27.6 %collective-permute-start.8 = (bf16[1,2,64,768]{3,2,1,0:T(8,128)(2,1)S(1)}, bf16[1,2,64,768]{3,2,1,0:T(8,128)(2,1)S(1)}, u32[]{:S(2)}, u32[]{:S(2)}) collective-permute-start(bf16[1,2,64,768]{3,2,1,0:T(8,128)(2,1)S(1)} %copy-done.7), channel_id=1, source_target_pairs={{0,9},{1,8},{2,11},{3,10},{4,13},{5,12},{6,15},{7,14},{8,1},{9,0},... | collective-permute-start | bytes 589832 | tf_op jit(solution)/shard_map/ppermute | solution.py:18
  219.7 20.9 %collective-permute-start.9 = (bf16[1,2,64,768]{3,2,1,0:T(8,128)(2,1)S(1)}, bf16[1,2,64,768]{3,2,1,0:T(8,128)(2,1)S(1)}, u32[]{:S(2)}, u32[]{:S(2)}) collective-permute-start(bf16[1,2,64,768]{3,2,1,0:T(8,128)(2,1)S(1)} %copy-done.6), channel_id=1, source_target_pairs={{0,10},{1,11},{2,8},{3,9},{4,14},{5,15},{6,12},{7,13},{8,2},{9,3},... | collective-permute-start | bytes 589832 | tf_op jit(solution)/shard_map/ppermute | solution.py:18
  228.4 15.6 %collective-permute-start.10 = (bf16[1,2,64,768]{3,2,1,0:T(8,128)(2,1)S(1)}, bf16[1,2,64,768]{3,2,1,0:T(8,128)(2,1)S(1)}, u32[]{:S(2)}, u32[]{:S(2)}) collective-permute-start(bf16[1,2,64,768]{3,2,1,0:T(8,128)(2,1)S(1)} %copy-done.5), channel_id=1, source_target_pairs={{0,11},{1,10},{2,9},{3,8},{4,15},{5,14},{6,13},{7,12},{8,3},{9,2},... | collective-permute-start | bytes 589832 | tf_op jit(solution)/shard_map/ppermute | solution.py:18
  228.6 17.2 %collective-permute-start.11 = (bf16[1,2,64,768]{3,2,1,0:T(8,128)(2,1)S(1)}, bf16[1,2,64,768]{3,2,1,0:T(8,128)(2,1)S(1)}, u32[]{:S(2)}, u32[]{:S(2)}) collective-permute-start(bf16[1,2,64,768]{3,2,1,0:T(8,128)(2,1)S(1)} %copy-done.4), channel_id=1, source_target_pairs={{0,12},{1,13},{2,14},{3,15},{4,8},{5,9},{6,10},{7,11},{8,4},{9,5},... | collective-permute-start | bytes 589832 | tf_op jit(solution)/shard_map/ppermute | solution.py:18
  228.7 17.1 %collective-permute-start.12 = (bf16[1,2,64,768]{3,2,1,0:T(8,128)(2,1)S(1)}, bf16[1,2,64,768]{3,2,1,0:T(8,128)(2,1)S(1)}, u32[]{:S(2)}, u32[]{:S(2)}) collective-permute-start(bf16[1,2,64,768]{3,2,1,0:T(8,128)(2,1)S(1)} %copy-done.3), channel_id=1, source_target_pairs={{0,13},{1,12},{2,15},{3,14},{4,9},{5,8},{6,11},{7,10},{8,5},{9,4},... | collective-permute-start | bytes 589832 | tf_op jit(solution)/shard_map/ppermute | solution.py:18
  232.7 15.3 %collective-permute-start.13 = (bf16[1,2,64,768]{3,2,1,0:T(8,128)(2,1)S(1)}, bf16[1,2,64,768]{3,2,1,0:T(8,128)(2,1)S(1)}, u32[]{:S(2)}, u32[]{:S(2)}) collective-permute-start(bf16[1,2,64,768]{3,2,1,0:T(8,128)(2,1)S(1)} %copy-done.2), channel_id=1, source_target_pairs={{0,14},{1,15},{2,12},{3,13},{4,10},{5,11},{6,8},{7,9},{8,6},{9,7},... | collective-permute-start | bytes 589832 | tf_op jit(solution)/shard_map/ppermute | solution.py:18
  240.5 9.5 %collective-permute-start.14 = (bf16[1,2,64,768]{3,2,1,0:T(8,128)(2,1)S(1)}, bf16[1,2,64,768]{3,2,1,0:T(8,128)(2,1)S(1)}, u32[]{:S(2)}, u32[]{:S(2)}) collective-permute-start(bf16[1,2,64,768]{3,2,1,0:T(8,128)(2,1)S(1)} %get-tuple-element.18), channel_id=1, source_target_pairs={{0,15},{1,14},{2,13},{3,12},{4,11},{5,10},{6,9},{7,8},{8,7},{9,6},... | collective-permute-start | bytes 589832 | tf_op jit(solution)/shard_map/ppermute | solution.py:18
  341.5 0.7 copy-start.12
  341.5 1.9 copy-start
Sparse Core Ops, SparseCore 0:
  9.8 48.9 all-gather.1
  341.6 127.8 all-reduce.4
